TPU v7x, 256 devices: a whole 4x4x8 slice. The times are simulated.
256 devices in a mesh: slab: 128 (over z, y_lo, x, core), plane: 2 (over y_hi).
Axes of the slice: x: 4, y: 4 (y_hi: 2, y_lo: 2; y = y_hi * 2 + y_lo), z: 8, core: 2. Of those that a mesh axis runs over, the one named last changes fastest.
Arguments:
- probe_pos: bfloat16 [3, 32768], P(None, ('slab', 'plane')), may hold values from 0 to 2
- atom_pos: bfloat16 [3, 32768], P(None, ('slab', 'plane')), may hold values from 0 to 2
- atom_feat: bfloat16 [128, 32768], P(None, ('slab', 'plane')), may hold values from -6 to 6
- neighbours: int32 [32, 32768], P(None, ('slab', 'plane')), may hold values from 0 to 32767, as said below
- valid: int32 [32, 32768], P(None, ('slab', 'plane')), may hold values 0 or 1
- w_radial1: float32 [64, 8], replicated, may hold values from -2 to 2
- w_radial2: bfloat16 [640, 64], replicated, may hold values from -0.75 to 0.75
- readout: float32 [5, 128], replicated, may hold values from -0.5 to 0.5
- cotangent: float32 [32768], P(('slab', 'plane')), may hold values from -6 to 6
Outputs:
- density: float32 [32768], P(('slab', 'plane'))
- grad_feat: float32 [128, 32768], P(None, ('slab', 'plane'))
- grad_radial1: float32 [64, 8], replicated
- grad_radial2: float32 [640, 64], replicated
- grad_readout: float32 [5, 128], replicated
Inputs may be any that keep to these rules, and one draw needn't show every extreme that they name: `neighbours`: the atom of every slot of probe p lies in the slab of p (atoms a with a // 256 = p // 256) or in one of the two slabs beside it on the periodic cycle of slabs.
All inputs are finite; a program needn't handle non-finite values. No bound on the sum of `valid` on one device may be relied on, other than what follows from the above.
Results may differ from a plain program's by a relative error of at most 0.0049.
Values may be sent and summed in bfloat16 or wider, within the bound.
No kernel may reach another device: no remote copies, remote signals or barrier semaphores. Data moves between devices by JAX's collectives and lax.ppermute only.
A program may use at most 128 MiB of HBM per device.

v0:
```python
import math
import jax
import jax.numpy as jnp
from jax import lax
from jax.sharding import PartitionSpec as P

slab_width = 2.0
soften = 0.25


def padded(block, sides, width):
    for axis, dim in sides:
        count = lax.axis_size(axis)
        forward = [(i, i + 1) for i in range(count - 1)]
        forward.append((count - 1, 0))
        backward = [(target, source) for source, target in forward]
        low = lax.ppermute(
            lax.slice_in_dim(block, block.shape[dim] - width, None, axis=dim), axis, forward
        )
        high = lax.ppermute(lax.slice_in_dim(block, 0, width, axis=dim), axis, backward)
        block = jnp.concatenate([low, block, high], axis=dim)
    return block


def passed_along(block, axis, distance):
    devices = range(lax.axis_size(axis))
    route = [((i - distance) % len(devices), i) for i in devices]
    return lax.ppermute(block, axis, route)


def harmonics(along_x, along_y, along_z):
    sq_x = along_x * along_x
    sq_y = along_y * along_y
    sq_z = along_z * along_z
    root3 = math.sqrt(3.0)
    root15 = math.sqrt(15.0)
    root5 = math.sqrt(5.0)
    coef_a1 = math.sqrt(35.0 / 8.0)
    coef_a2 = math.sqrt(105.0)
    coef_a3 = math.sqrt(21.0 / 8.0)
    coef_a4 = math.sqrt(7.0) / 2.0
    coef_b1 = 3.0 * math.sqrt(35.0) / 2.0
    coef_b2 = 3.0 * math.sqrt(70.0) / 4.0
    coef_b3 = 3.0 * math.sqrt(5.0) / 2.0
    coef_b4 = 3.0 * math.sqrt(10.0) / 4.0
    rows_out = [
        jnp.ones_like(along_x),
        root3 * along_y,
        root3 * along_z,
        root3 * along_x,
        root15 * along_x * along_y,
        root15 * along_y * along_z,
        root5 / 2.0 * (3.0 * sq_z - 1.0),
        root15 * along_x * along_z,
        root15 / 2.0 * (sq_x - sq_y),
        coef_a1 * along_y * (3.0 * sq_x - sq_y),
        coef_a2 * along_x * along_y * along_z,
        coef_a3 * along_y * (5.0 * sq_z - 1.0),
        coef_a4 * along_z * (5.0 * sq_z - 3.0),
        coef_a3 * along_x * (5.0 * sq_z - 1.0),
        coef_a2 / 2.0 * along_z * (sq_x - sq_y),
        coef_a1 * along_x * (sq_x - 3.0 * sq_y),
        coef_b1 * along_x * along_y * (sq_x - sq_y),
        coef_b2 * along_y * along_z * (3.0 * sq_x - sq_y),
        coef_b3 * along_x * along_y * (7.0 * sq_z - 1.0),
        coef_b4 * along_y * along_z * (7.0 * sq_z - 3.0),
        0.375 * (35.0 * sq_z * sq_z - 30.0 * sq_z + 3.0),
        coef_b4 * along_x * along_z * (7.0 * sq_z - 3.0),
        coef_b3 / 2.0 * (sq_x - sq_y) * (7.0 * sq_z - 1.0),
        coef_b2 * along_x * along_z * (sq_x - 3.0 * sq_y),
        coef_b1 / 4.0 * (sq_x * (sq_x - 3.0 * sq_y) - sq_y * (3.0 * sq_x - sq_y)),
    ]
    return jnp.stack(rows_out)


def probe_block(
    features, atom_xyz, probe_xyz, offset, weight_mask, cot_block, w_radial1, w_radial2, readout
):
    slots, block_len = weight_mask.shape
    edge_count = slots * block_len
    channels = features.shape[0]
    degrees = readout.shape[0]
    probe_tile = jnp.broadcast_to(probe_xyz[:, None, :], (3, slots, block_len)).reshape(
        3, edge_count
    )
    delta_x = atom_xyz[0] - probe_tile[0]
    delta_y = atom_xyz[1] - probe_tile[1]
    delta_z = atom_xyz[2] + slab_width * offset.reshape(edge_count) - probe_tile[2]
    radius = jnp.sqrt(delta_x * delta_x + delta_y * delta_y + delta_z * delta_z + soften)
    sphere = harmonics(delta_x / radius, delta_y / radius, delta_z / radius)
    centres = 0.75 * jnp.arange(w_radial1.shape[1], dtype=jnp.float32)
    radial_basis = jnp.exp(-2.0 * (radius[None, :] - centres[:, None]) ** 2)
    preact = jnp.dot(w_radial1, radial_basis, precision=lax.Precision.HIGHEST)
    hidden = jax.nn.silu(preact).astype(jnp.bfloat16)
    radial = jnp.dot(w_radial2, hidden, preferred_element_type=jnp.float32).reshape(
        degrees, channels, edge_count
    )
    weight = weight_mask.reshape(edge_count) * (1.0 / math.sqrt(slots))
    feat_float = features.astype(jnp.float32)
    messages = (radial * feat_float[None] * weight[None, None, :]).reshape(
        degrees, channels, slots, block_len
    )
    sphere_rows = sphere.reshape(degrees * degrees, slots, block_len)
    density = jnp.zeros((block_len,), jnp.float32)
    grad_msg = []
    grad_read = []
    for degree in range(degrees):
        part_y = sphere_rows[degree * degree : (degree + 1) * (degree + 1)]
        moment = jnp.einsum(
            "kjp,cjp->kcp", part_y, messages[degree], precision=lax.Precision.HIGHEST
        )
        if degree == 0:
            density = jnp.sum(readout[0][:, None] * moment[0], axis=0)
            grad_mom = cot_block[None, None, :] * readout[0][None, :, None]
            grad_read.append(jnp.sum(cot_block[None, :] * moment[0], axis=1))
        else:
            squares = jnp.sum(moment * moment, axis=0)
            density = density + jnp.sum(readout[degree][:, None] * squares, axis=0)
            grad_mom = 2.0 * cot_block[None, None, :] * readout[degree][None, :, None] * moment
            grad_read.append(jnp.sum(cot_block[None, :] * squares, axis=1))
        grad_msg.append(
            jnp.einsum("kjp,kcp->cjp", part_y, grad_mom, precision=lax.Precision.HIGHEST)
        )
    grad_messages = jnp.stack(grad_msg).reshape(degrees, channels, edge_count)
    grad_features = jnp.sum(grad_messages * radial, axis=0) * weight[None, :]
    grad_radial = (
        (grad_messages * feat_float[None] * weight[None, None, :])
        .reshape(degrees * channels, edge_count)
        .astype(jnp.bfloat16)
    )
    grad_w2 = lax.dot_general(
        grad_radial, hidden, (((1,), (1,)), ((), ())), preferred_element_type=jnp.float32
    )
    grad_hidden = lax.dot_general(
        w_radial2, grad_radial, (((0,), (0,)), ((), ())), preferred_element_type=jnp.float32
    )
    logistic = jax.nn.sigmoid(preact)
    grad_pre = grad_hidden * logistic * (1.0 + preact * (1.0 - logistic))
    grad_w1 = lax.dot_general(
        grad_pre, radial_basis, (((1,), (1,)), ((), ())), precision=lax.Precision.HIGHEST
    )
    return (density, grad_features, grad_w1, grad_w2, jnp.stack(grad_read))


def shards(
    probe_pos, atom_pos, atom_feat, neighbours, valid, w_radial1, w_radial2, readout, cotangent
):
    channels = atom_feat.shape[0]
    atom_dev = atom_feat.shape[1]
    plane_count = lax.axis_size("plane")
    slab_count = lax.axis_size("slab")
    slab_index = lax.axis_index("slab")
    atom_slab = atom_dev * plane_count
    atom_pack = jnp.concatenate([atom_feat, atom_pos], axis=0)
    slab_pack = lax.all_gather(atom_pack, "plane", axis=1, tiled=True)
    window = padded(slab_pack, (("slab", 1),), atom_slab)
    window_feat = window[:channels]
    window_xyz = window[channels:]
    local_rows = (neighbours - (slab_index - 1) * atom_slab) % (slab_count * atom_slab)
    offsets = (local_rows // atom_slab - 1).astype(jnp.float32)
    slots, probe_dev = neighbours.shape
    block_len = 128
    count = probe_dev // block_len
    rows_blocks = local_rows.reshape(slots, count, block_len).transpose(1, 0, 2)
    offset_blocks = offsets.reshape(slots, count, block_len).transpose(1, 0, 2)
    mask_blocks = valid.astype(jnp.float32).reshape(slots, count, block_len).transpose(1, 0, 2)
    probe_blocks = probe_pos.astype(jnp.float32).reshape(3, count, block_len).transpose(1, 0, 2)
    cot_blocks = cotangent.reshape(count, block_len)

    def advance(totals, inputs):
        grad_window, total_w1, total_w2, total_read = totals
        atom_rows, offset, mask_float, probe_xyz, cot_block = inputs
        flat_rows = atom_rows.reshape(-1)
        features = jnp.take(window_feat, flat_rows, axis=1)
        atom_xyz = jnp.take(window_xyz, flat_rows, axis=1).astype(jnp.float32)
        density, grad_features, grad_w1, grad_w2, grad_read = probe_block(
            features,
            atom_xyz,
            probe_xyz,
            offset,
            mask_float,
            cot_block,
            w_radial1,
            w_radial2,
            readout,
        )
        grad_window = grad_window.at[:, flat_rows].add(grad_features)
        return (
            (grad_window, total_w1 + grad_w1, total_w2 + grad_w2, total_read + grad_read),
            density,
        )

    start_totals = (
        jnp.zeros((channels, 3 * atom_slab), jnp.float32),
        jnp.zeros(w_radial1.shape, jnp.float32),
        jnp.zeros(w_radial2.shape, jnp.float32),
        jnp.zeros(readout.shape, jnp.float32),
    )
    totals, densities = lax.scan(
        advance, start_totals, (rows_blocks, offset_blocks, mask_blocks, probe_blocks, cot_blocks)
    )
    grad_window = totals[0]
    lower_part = passed_along(grad_window[:, :atom_slab], "slab", -1)
    upper_part = passed_along(grad_window[:, 2 * atom_slab :], "slab", 1)
    owned_part = grad_window[:, atom_slab : 2 * atom_slab] + lower_part + upper_part
    grad_feat = lax.psum_scatter(owned_part, "plane", scatter_dimension=1, tiled=True)
    summed_w1, summed_w2, summed_read = lax.psum(
        (totals[1], totals[2], totals[3]), ("slab", "plane")
    )
    scale = 1.0 / math.sqrt(probe_dev * slab_count * plane_count)
    return (
        densities.reshape(-1),
        grad_feat,
        summed_w1 * scale,
        summed_w2 * scale,
        summed_read * scale,
    )


def solution(mesh):
    in_specs = (
        P(None, ("slab", "plane")),
        P(None, ("slab", "plane")),
        P(None, ("slab", "plane")),
        P(None, ("slab", "plane")),
        P(None, ("slab", "plane")),
        P(),
        P(),
        P(),
        P(("slab", "plane")),
    )
    out_specs = (P(("slab", "plane")), P(None, ("slab", "plane")), P(), P(), P())
    return jax.shard_map(shards, mesh=mesh, in_specs=in_specs, out_specs=out_specs, check_vma=False)
```

profile of v0, /device:TPU:1, one launch (start us, length us, event | category | flops | bytes accessed | tf_op | source)
XLA Modules:
  0.0 536.8 jit_solution(2991363688126804630)
XLA Ops:
  9.8 6.0 %all_gather.3 = bf16[131,256]{0,1:T(8,128)(2,1)S(1)} all-gather(bf16[131,128]{0,1:T(8,128)(2,1)S(1)} %pad_maximum_fusion), channel_id=1, replica_groups=mesh['slab'=128,'plane'=2] {'plane'}, dimensions={1}, use_global_device_ids=true | all-gather | bytes 100608 | tf_op jit(solution)/shard_map/all_gather | solution.py:155
  15.8 3.0 collective-permute-start
  24.4 12.1 %gather_fusion = bf16[4096,3]{1,0:T(8,128)(2,1)S(1)} fusion(bf16[3,768]{0,1:T(8,128)(2,1)S(1)} %slice.163, s32[4096]{0:T(1024)S(1)} %broadcast_clamp_fusion), kind=kCustom, calls=%fused_computation | custom fusion | bytes 65536 | tf_op jit(solution)/shard_map/while/body/eval_jaxpr/jit(_take)/gather | solution.py:175
  41.3 5.4 %fusion.59 = f32[4096,640]{0,1:T(8,128)} fusion(bf16[640,64]{0,1:T(8,128)(2,1)S(1)} %copy-done, f32[64,4096]{1,0:T(8,128)S(1)} %convolution_bitcast_fusion.1), kind=kOutput, calls=%fused_computation.167 | convolution fusion | flops 336855040 | bytes 11616256 | tf_op jit(solution)/shard_map/while/body/eval_jaxpr/dot_general | solution.py:95
  46.8 11.3 %copy.168 = f32[5,128,4096]{1,2,0:T(8,128)} copy(f32[5,128,4096]{2,1,0:T(8,128)} %bitcast.125) | data formatting | bytes 20971520 | tf_op jit(solution)/shard_map/while/body/eval_jaxpr/reshape | solution.py:95
  58.0 14.9 %gather_fusion.1 = bf16[4096,128]{1,0:T(8,128)(2,1)} fusion(bf16[128,768]{0,1:T(8,128)(2,1)S(1)} %slice.167, s32[4096]{0:T(1024)S(1)} %broadcast_clamp_fusion), kind=kCustom, calls=%fused_computation.1 | custom fusion | bytes 2113536 | tf_op jit(solution)/shard_map/while/body/eval_jaxpr/jit(_take)/gather | solution.py:174
  72.9 3.4 convert_bitcast_fusion
  76.3 5.8 %multiply_multiply_fusion = f32[5,128,4096]{1,2,0:T(8,128)S(1)} fusion(f32[5,128,4096]{1,2,0:T(8,128)} %copy.168, f32[4096]{0:T(1024)S(1)} %multiply_bitcast_fusion.1, f32[128,4096]{0,1:T(8,128)S(1)} %convert_bitcast_fusion), kind=kLoop, calls=%fused_computation.6 | loop fusion | flops 5242880 | bytes 23085056 | tf_op jit(solution)/shard_map/while/body/eval_jaxpr/mul | solution.py:100
  82.1 4.0 fusion.61
  86.1 5.2 fusion.5
  94.6 1.9 copy.172
  96.5 1.6 stack.108
  99.7 1.9 copy.174
  101.6 4.8 multiply_reduce_fusion.1
  106.5 3.1 multiply_reduce_fusion.4
  109.7 3.3 multiply_reduce_fusion.3
  113.1 3.1 multiply_reduce_fusion.2
  116.9 3.5 convolution_bitcast_fusion.5
  121.6 3.9 convolution_bitcast_fusion.4
  126.7 3.5 convolution_bitcast_fusion.3
  131.4 3.5 convolution_bitcast_fusion.2
  139.1 7.6 %broadcast_multiply_fusion = (f32[5,128,4096]{1,2,0:T(8,128)}, f32[128,4096]{0,1:T(8,128)}) fusion(f32[5,128,4096]{1,2,0:T(8,128)S(1)} %constant_dynamic-update-slice_fusion.3, f32[128,4096]{0,1:T(8,128)S(1)} %convert_bitcast_fusion, f32[5,128,4096]{1,2,0:T(8,128)S(1)} %bitcast.124), kind=kLoop, calls=%fused_computation.7 | loop fusion | flops 7340032 | bytes 35651584 | tf_op jit(solution)/shard_map/while/body/eval_jaxpr/mul | solution.py:127
  146.7 11.3 %copy.186 = f32[5,128,4096]{2,1,0:T(8,128)} copy(f32[5,128,4096]{1,2,0:T(8,128)} %get-tuple-element.109) | data formatting | bytes 20971520 | tf_op jit(solution)/shard_map/while/body/eval_jaxpr/mul | solution.py:127
  158.0 5.4 %fusion = bf16[640,4096]{1,0:T(8,128)(2,1)S(1)} fusion(f32[5,128,4096]{2,1,0:T(8,128)} %copy.186, f32[4096]{0:T(1024)S(1)} %multiply_bitcast_fusion.1), kind=kLoop, calls=%fused_computation.4 | loop fusion | flops 5242880 | bytes 15745024 | tf_op jit(solution)/shard_map/while/body/eval_jaxpr/convert_element_type | solution.py:129
  163.3 2.1 fusion.2
  165.5 2.4 fusion.58
  167.9 24.6 %scatter_custom_fusion = f32[128,768]{0,1:T(8,128)S(1)} fusion(s32[4096]{0:T(1024)} %bitcast.154, f32[128,4096]{0,1:T(8,128)S(1)} %copy-done.4, f32[4096]{0:T(1024)S(1)} %multiply_bitcast_fusion.1, f32[]{:T(128)} %constant.170.clone.1), kind=kCustom, calls=%fused_computation.12 | custom fusion | flops 1048576 | bytes 2507264 | tf_op jit(solution)/shard_map/while/body/eval_jaxpr/scatter-add | solution.py:187
  193.7 4.9 collective-permute-start.2
  198.6 2.2 fusion.39
  200.9 80.1 %all-reduce = (f32[64,8]{0,1:T(8,128)S(1)}, f32[5,128]{1,0:T(8,128)S(1)}) all-reduce(f32[64,8]{0,1:T(8,128)S(1)} %fusion.39, f32[5,128]{1,0:T(8,128)S(1)} %stack.121), channel_id=1, replica_groups=mesh['slab'=128,'plane'=2] {'slab','plane'}, use_global_device_ids=true, to_apply=%region_12.13 | all-reduce | flops 1152 | bytes 9216 | tf_op jit(solution)/shard_map/psum | solution.py:207
  283.4 242.6 %all-reduce.3.cloned.1.call-done = f32[640,64]{0,1:T(8,128)} async-done(((f32[640,64]{0,1:T(8,128)}), f32[640,64]{0,1:T(8,128)}) %all-reduce.3.cloned.1.call-update) | async-done | bytes 163856 | tf_op jit(solution)/shard_map/psum | solution.py:207
  526.0 1.6 broadcast_multiply_fusion.1
  (119 shorter events, 30.6 us)
Async XLA Ops:
  8.0 33.3 %copy-start = (bf16[640,64]{0,1:T(8,128)(2,1)S(1)}, bf16[640,64]{0,1:T(8,128)(2,1)}, u32[]{:S(2)}) copy-start(bf16[640,64]{0,1:T(8,128)(2,1)} %param.15) | copy-start | bytes 245764
  8.0 518.0 %all-reduce.3.cloned.1.call-start = ((), (), s32[]{:S(2)}) async-start(), calls=%async_computation.2 | async-start | bytes 327680 | tf_op jit(solution)/shard_map/psum | solution.py:207
  15.8 8.4 %collective-permute-start = (bf16[131,256]{0,1:T(8,128)(2,1)S(1)}, bf16[131,256]{0,1:T(8,128)(2,1)S(1)}, u32[]{:S(2)}, u32[]{:S(2)}) collective-permute-start(bf16[131,256]{0,1:T(8,128)(2,1)S(1)} %all_gather.3), channel_id=1, source_target_pairs={{0,2},{2,4},{4,6},{6,8},{8,10},{10,12},{12,14},{14,16},{16,18},{18... | collective-permute-start | bytes 201224 | tf_op jit(solution)/shard_map/ppermute | solution.py:17
  18.8 5.5 %collective-permute-start.1 = (bf16[131,256]{0,1:T(8,128)(2,1)S(1)}, bf16[131,256]{0,1:T(8,128)(2,1)S(1)}, u32[]{:S(2)}, u32[]{:S(2)}) collective-permute-start(bf16[131,256]{0,1:T(8,128)(2,1)S(1)} %all_gather.3), channel_id=1, source_target_pairs={{2,0},{4,2},{6,4},{8,6},{10,8},{12,10},{14,12},{16,14},{18,16},{20... | collective-permute-start | bytes 201224 | tf_op jit(solution)/shard_map/ppermute | solution.py:20
  20.9 3.4 copy-start.12
  24.2 16.0 %copy-start.14 = (f32[8]{0:T(128)}, f32[8]{0:T(128)S(1)}, u32[]{:S(2)}) copy-start(f32[8]{0:T(128)S(1)} %iota_multiply_fusion) | copy-start | bytes 100
  36.5 3.8 copy-start.13
  38.5 8.3 %copy-start.10 = (f32[1,4096]{1,0:T(1,128)}, f32[1,4096]{1,0:T(1,128)S(1)}, u32[]{:S(2)}) copy-start(f32[1,4096]{1,0:T(1,128)S(1)} %get-tuple-element.150) | copy-start | bytes 49156
  41.3 5.4 %copy-start.5 = (f32[64,4096]{1,0:T(8,128)}, f32[64,4096]{1,0:T(8,128)S(1)}, u32[]{:S(2)}) copy-start(f32[64,4096]{1,0:T(8,128)S(1)} %convolution_bitcast_fusion.1) | copy-start | bytes 3145732
  101.6 4.9 copy-start.3
  106.5 3.2 copy-start.2
  106.5 3.2 copy-start.7
  109.6 3.4 copy-start.1
  109.6 3.4 copy-start.8
  113.0 3.2 copy-start.9
  113.0 3.2 copy-start.16
  113.0 3.2 copy-start.17
  113.0 3.2 copy-start.18
  113.0 3.2 copy-start.19
  113.0 3.2 copy-start.20
  113.0 3.2 copy-start.21
  113.1 3.2 copy-start.22
  134.9 2.2 slice-start
  136.1 2.5 slice-start.1
  136.6 2.5 slice-start.2
  157.9 5.4 %copy-start.6 = (f32[64,4096]{1,0:T(8,128)S(1)}, f32[64,4096]{1,0:T(8,128)}, u32[]{:S(2)}) copy-start(f32[64,4096]{1,0:T(8,128)} %copy-done.5) | copy-start | bytes 3145732
  165.5 2.4 copy-start.4
  167.9 30.7 %copy-start.11 = (f32[1,4096]{1,0:T(1,128)S(1)}, f32[1,4096]{1,0:T(1,128)}, u32[]{:S(2)}) copy-start(f32[1,4096]{1,0:T(1,128)} %copy-done.10) | copy-start | bytes 49156
  167.9 30.7 %copy-start.15 = (f32[8]{0:T(128)S(1)}, f32[8]{0:T(128)}, u32[]{:S(2)}) copy-start(f32[8]{0:T(128)} %copy-done.14) | copy-start | bytes 100
  192.5 89.7 %collective-permute-start.3 = (f32[128,256]{0,1:T(8,128)S(1)}, f32[128,256]{0,1:T(8,128)S(1)}, u32[]{:S(2)}, u32[]{:S(2)}) collective-permute-start(f32[128,256]{0,1:T(8,128)S(1)} %get-tuple-element.117), channel_id=1, source_target_pairs={{254,0},{0,2},{2,4},{4,6},{6,8},{8,10},{10,12},{12,14},{14,16},{16... | collective-permute-start | bytes 393224 | tf_op jit(solution)/shard_map/ppermute | solution.py:28
  193.7 88.5 %collective-permute-start.2 = (f32[128,256]{0,1:T(8,128)S(1)}, f32[128,256]{0,1:T(8,128)S(1)}, u32[]{:S(2)}, u32[]{:S(2)}) collective-permute-start(f32[128,256]{0,1:T(8,128)S(1)} %get-tuple-element.116), channel_id=1, source_target_pairs={{2,0},{4,2},{6,4},{8,6},{10,8},{12,10},{14,12},{16,14},{18,16},{20... | collective-permute-start | bytes 393224 | tf_op jit(solution)/shard_map/ppermute | solution.py:28
  281.6 246.1 %reduce-scatter.2.cloned.1.call-start = ((), (), s32[]{:S(2)}) async-start(), calls=%async_computation.1 | async-start | bytes 196608 | tf_op jit(solution)/shard_map/reduce_scatter | solution.py:206
Sparse Core Ops, SparseCore 0:
  281.7 244.2 all-reduce.2
Sparse Core Ops, SparseCore 1:
  284.5 12.7 reduce-scatter.1
where the time goes:
time: 544 us; the launch traced here: 537 us
  waiting for transfers between devices  243 us (45%)
  blocking collectives  86.1 us (16%)
  local copies, waits for them, and re-layouts  78.1 us (14%)
  other arithmetic  56.8 us (10%)
  matrix products  47 us (9%)
  between operations  16.3 us (3%)
  starting transfers between devices  9.81 us (2%)
    psum x1, waiting for transfers between devices, shards(): lax.psum((totals[1], totals[2], totals[3]), ('slab', 'plane'))  243 us
    psum x1, blocking collectives, shards(): lax.psum((totals[1], totals[2], totals[3]), ('slab', 'plane'))  80.1 us
    scatter-add x1, other arithmetic, advance(): grad_window = grad_window.at[:, flat_rows].add(grad_features)  24.6 us
    dot_general x5, matrix products, probe_block(): jnp.einsum('kjp,cjp->kcp', part_y, messages[degree], precision=lax.Precis...  19.5 us
    gather x1, local copies, waits for them, and re-layouts, advance(): features = jnp.take(window_feat, flat_rows, axis=1)  14.9 us
    dot_general x4, matrix products, probe_block(): jnp.einsum('kjp,kcp->cjp', part_y, grad_mom, precision=lax.Precision.HIGH...  14.3 us
    gather x2, local copies, waits for them, and re-layouts, advance(): atom_xyz = jnp.take(window_xyz, flat_rows, axis=1).astype(jnp.float32)  12.5 us
    mul x1, local copies, waits for them, and re-layouts, probe_block(): grad_messages * feat_float[None] * weight[None, None, :]  11.3 us
  transfers between devices with their start and end apart: 6, of which 1 were waited for; matrix products, arithmetic and copies ran while one was open for 2% of the time, Pallas kernels for 0%

commit v1 on v0

--- a/solution.py
+++ b/solution.py
@@ -205,7 +205,7 @@
     owned_part = grad_window[:, atom_slab : 2 * atom_slab] + lower_part + upper_part
     grad_feat = lax.psum_scatter(owned_part, "plane", scatter_dimension=1, tiled=True)
     summed_w1, summed_w2, summed_read = lax.psum(
-        (totals[1], totals[2], totals[3]), ("slab", "plane")
+        lax.psum((totals[1], totals[2], totals[3]), axis_name="slab"), axis_name="plane"
     )
     scale = 1.0 / math.sqrt(probe_dev * slab_count * plane_count)
     return (

time: 544 us -> 1510 us (2.78)
  waiting for transfers between devices: 243 us -> 1000 us
  blocking collectives: 86.1 us -> 296 us
    psum x1 -> x2, waiting for transfers between devices: 243 us -> 984 us  [the longest x1 951 us: shards(): lax.psum((totals[1], totals[2], totals[3]), axis_name='slab')]
    psum x1 -> x2, blocking collectives: 80.1 us -> 290 us  [the longest x1 285 us: shards(): lax.psum((totals[1], totals[2], totals[3]), axis_name='slab')]
    reduce_scatter x1, waiting for transfers between devices: 0.01 us -> 17.6 us  [shards(): lax.psum_scatter(owned_part, 'plane', scatter_dimension=1, tiled=True)]
  transfers between devices with their start and end apart: 6 -> 7, of which waited for: 1 -> 3; matrix products, arithmetic and copies ran while one was open for 2% -> 1% of each run, Pallas kernels for 0% -> 0%
where the time goes in v1:
time: 1510 us; the launch traced here: 1500 us
  waiting for transfers between devices  1000 us (66%)
  blocking collectives  296 us (20%)
  local copies, waits for them, and re-layouts  78.1 us (5%)
  other arithmetic  56.8 us (4%)
  matrix products  47 us (3%)
    psum x1, waiting for transfers between devices, shards(): lax.psum((totals[1], totals[2], totals[3]), axis_name='slab')  951 us
    psum x1, blocking collectives, shards(): lax.psum((totals[1], totals[2], totals[3]), axis_name='slab')  285 us
    psum x1, waiting for transfers between devices, shards(): lax.psum(lax.psum((totals[1], totals[2], totals[3]), axis_name='slab'), a...  32.7 us
  transfers between devices with their start and end apart: 7, of which 3 were waited for; matrix products, arithmetic and copies ran while one was open for 1% of the time, Pallas kernels for 0%

profile of v1, /device:TPU:1, one launch (start us, length us, event | category | flops | bytes accessed | tf_op | source)
XLA Modules:
  0.0 1503.8 jit_solution(13497812239149530609)
XLA Ops:
  8.9 6.0 all_gather.3
  15.0 3.0 collective-permute-start
  23.5 12.1 gather_fusion
  40.5 5.4 fusion.59
  45.9 11.3 copy.168
  57.2 14.9 gather_fusion.1
  72.1 3.4 convert_bitcast_fusion
  75.4 5.8 multiply_multiply_fusion
  81.3 4.0 fusion.61
  85.3 5.2 fusion.5
  98.9 1.9 copy.174
  100.8 4.8 multiply_reduce_fusion.1
  105.7 3.1 multiply_reduce_fusion.4
  108.8 3.3 multiply_reduce_fusion.3
  112.3 3.1 multiply_reduce_fusion.2
  116.1 3.5 convolution_bitcast_fusion.5
  120.8 3.9 convolution_bitcast_fusion.4
  125.8 3.5 convolution_bitcast_fusion.3
  130.5 3.5 convolution_bitcast_fusion.2
  138.3 7.6 broadcast_multiply_fusion
  145.8 11.3 copy.186
  157.1 5.4 fusion
  162.5 2.1 fusion.2
  164.7 2.4 fusion.58
  167.0 24.6 %scatter_custom_fusion = f32[128,768]{0,1:T(8,128)S(1)} fusion(s32[4096]{0:T(1024)} %bitcast.154, f32[128,4096]{0,1:T(8,128)S(1)} %copy-done.4, f32[4096]{0:T(1024)S(1)} %multiply_bitcast_fusion.1, f32[]{:T(128)} %constant.170.clone.1), kind=kCustom, calls=%fused_computation.12 | custom fusion | flops 1048576 | bytes 2507264 | tf_op jit(solution)/shard_map/while/body/eval_jaxpr/scatter-add | solution.py:187
  192.9 4.9 collective-permute-start.2
  197.8 2.2 fusion.39
  200.0 284.9 %all-reduce = (f32[64,8]{0,1:T(8,128)S(1)}, f32[5,128]{1,0:T(8,128)S(1)}) all-reduce(f32[64,8]{0,1:T(8,128)S(1)} %fusion.39, f32[5,128]{1,0:T(8,128)S(1)} %stack.121), channel_id=1, replica_groups=mesh['slab'=128,'plane'=2] {'slab'}, use_global_device_ids=true, to_apply=%region_12.13 | all-reduce | flops 1152 | bytes 9216 | tf_op jit(solution)/shard_map/psum | solution.py:208
  484.9 5.3 all-reduce.1
  491.5 950.8 %all-reduce.5.cloned.1.call-done = f32[640,64]{0,1:T(8,128)} async-done(((f32[640,64]{0,1:T(8,128)}), f32[640,64]{0,1:T(8,128)}) %all-reduce.5.cloned.1.call-update) | async-done | bytes 163856 | tf_op jit(solution)/shard_map/psum | solution.py:208
  1443.6 32.7 %all-reduce.7.cloned.1.call-done = f32[640,64]{0,1:T(8,128)} async-done(((f32[640,64]{0,1:T(8,128)}), f32[640,64]{0,1:T(8,128)}) %all-reduce.7.cloned.1.call-update) | async-done | bytes 163856 | tf_op jit(solution)/shard_map/psum | solution.py:207
  1477.9 17.6 %reduce-scatter.2.cloned.1.call-done = f32[128,128]{0,1:T(8,128)} async-done(((f32[128,256]{0,1:T(8,128)}), f32[128,128]{0,1:T(8,128)}) %reduce-scatter.2.cloned.1.call-update) | async-done | bytes 65552 | tf_op jit(solution)/shard_map/reduce_scatter | solution.py:206
  (123 shorter events, 35.8 us)
Async XLA Ops:
  7.2 33.3 %copy-start = (bf16[640,64]{0,1:T(8,128)(2,1)S(1)}, bf16[640,64]{0,1:T(8,128)(2,1)}, u32[]{:S(2)}) copy-start(bf16[640,64]{0,1:T(8,128)(2,1)} %param.15) | copy-start | bytes 245764
  7.2 1435.1 %all-reduce.5.cloned.1.call-start = ((), (), s32[]{:S(2)}) async-start(), calls=%async_computation.2 | async-start | bytes 327680 | tf_op jit(solution)/shard_map/psum | solution.py:208
  15.0 8.4 collective-permute-start
  18.0 5.5 collective-permute-start.1
  20.0 3.4 copy-start.12
  23.4 16.0 %copy-start.14 = (f32[8]{0:T(128)}, f32[8]{0:T(128)S(1)}, u32[]{:S(2)}) copy-start(f32[8]{0:T(128)S(1)} %iota_multiply_fusion) | copy-start | bytes 100
  35.7 3.8 copy-start.13
  37.7 8.3 copy-start.10
  40.5 5.4 copy-start.5
  100.8 4.9 copy-start.3
  105.6 3.2 copy-start.2
  105.7 3.2 copy-start.7
  108.8 3.4 copy-start.1
  108.8 3.4 copy-start.8
  112.1 3.2 copy-start.9
  112.2 3.2 copy-start.16
  112.2 3.2 copy-start.17
  112.2 3.2 copy-start.18
  112.2 3.2 copy-start.19
  112.2 3.2 copy-start.20
  112.2 3.2 copy-start.21
  112.2 3.2 copy-start.22
  135.3 2.5 slice-start.1
  135.8 2.5 slice-start.2
  157.1 5.4 copy-start.6
  164.7 2.4 copy-start.4
  167.0 30.7 %copy-start.11 = (f32[1,4096]{1,0:T(1,128)S(1)}, f32[1,4096]{1,0:T(1,128)}, u32[]{:S(2)}) copy-start(f32[1,4096]{1,0:T(1,128)} %copy-done.10) | copy-start | bytes 49156
  167.0 30.7 %copy-start.15 = (f32[8]{0:T(128)S(1)}, f32[8]{0:T(128)}, u32[]{:S(2)}) copy-start(f32[8]{0:T(128)} %copy-done.14) | copy-start | bytes 100
  191.7 1250.7 %collective-permute-start.3 = (f32[128,256]{0,1:T(8,128)S(1)}, f32[128,256]{0,1:T(8,128)S(1)}, u32[]{:S(2)}, u32[]{:S(2)}) collective-permute-start(f32[128,256]{0,1:T(8,128)S(1)} %get-tuple-element.119), channel_id=1, source_target_pairs={{254,0},{0,2},{2,4},{4,6},{6,8},{8,10},{10,12},{12,14},{14,16},{16... | collective-permute-start | bytes 393224 | tf_op jit(solution)/shard_map/ppermute | solution.py:28
  192.9 1249.5 %collective-permute-start.2 = (f32[128,256]{0,1:T(8,128)S(1)}, f32[128,256]{0,1:T(8,128)S(1)}, u32[]{:S(2)}, u32[]{:S(2)}) collective-permute-start(f32[128,256]{0,1:T(8,128)S(1)} %get-tuple-element.118), channel_id=1, source_target_pairs={{2,0},{4,2},{6,4},{8,6},{10,8},{12,10},{14,12},{16,14},{18,16},{20... | collective-permute-start | bytes 393224 | tf_op jit(solution)/shard_map/ppermute | solution.py:28
  490.9 985.5 %all-reduce.7.cloned.1.call-start = ((), (), s32[]{:S(2)}) async-start(), calls=%async_computation.3 | async-start | bytes 327680 | tf_op jit(solution)/shard_map/psum | solution.py:207
  1442.3 53.2 %reduce-scatter.2.cloned.1.call-start = ((), (), s32[]{:S(2)}) async-start(), calls=%async_computation.1 | async-start | bytes 196608 | tf_op jit(solution)/shard_map/reduce_scatter | solution.py:206
  (1 other events, 2.2 us)
Sparse Core Ops, SparseCore 0:
  491.0 951.2 all-reduce.4
  1444.8 31.4 all-reduce.6
  1478.8 16.6 reduce-scatter.1
